TPU v7x, 32 devices: a whole 2x2x4 slice. The times are simulated.
32 devices in a mesh: expert: 16 (over z, y, x), dp: 2 (over core).
Axes of the slice: x: 2, y: 2, z: 4, core: 2. Of those that a mesh axis runs over, the one named last changes fastest.
Arguments:
- tokens: bfloat16 [2, 256, 4096], P(None, ('expert', 'dp')), may hold values from -6 to 6
- norm_gain: float32 [4096], replicated, may hold values from 0.5 to 1.5
- route_ids: int32 [2, 256, 8], P(None, ('expert', 'dp')), may hold values from 0 to 15, all different within a row; in each aligned block of 8 rows (0 to 7, 8 to 15, ..., all dimensions but the last counted through in order) at most 8 rows name the same one
- route_weights: float32 [2, 256, 8], P(None, ('expert', 'dp')), may hold values from 0.05 to 0.25
- rows_left: int32 [256], P(('expert', 'dp')), may hold values from 1 to 40
- gate_up_elems: bfloat16 [16, 2, 4096, 1024], P('expert', None, None, 'dp'), may hold values from -0.09375 to 0.09375
- gate_up_scales: bfloat16 [16, 2, 128, 1024], P('expert', None, None, 'dp'), may hold values from 0.5 to 2, as said below
- down_elems: bfloat16 [16, 1024, 4096], P('expert', 'dp'), may hold values from -0.1875 to 0.1875
- down_scales: bfloat16 [16, 32, 4096], P('expert', 'dp'), may hold values from 0.5 to 2, as said below
- swap_pairs: int32 [8], replicated, may hold values 0 or 1
Outputs:
- mixed: bfloat16 [2, 256, 4096], P(None, ('expert', 'dp'))
- new_gate_up_elems: bfloat16 [16, 2, 4096, 1024], P('expert', None, None, 'dp')
- new_gate_up_scales: bfloat16 [16, 2, 128, 1024], P('expert', None, None, 'dp')
- new_down_elems: bfloat16 [16, 1024, 4096], P('expert', 'dp')
- new_down_scales: bfloat16 [16, 32, 4096], P('expert', 'dp')
Inputs may be any that keep to these rules, and one draw needn't show every extreme that they name: `route_ids`: within a step each row names 8 different experts; among the 8 rows of one device in a step, at most 8 name any one expert, and exactly 8 do for some expert. `gate_up_scales`: every entry is a power of two. `down_scales`: every entry is a power of two.
All inputs are finite; a program needn't handle non-finite values.
Results may differ from a plain program's by a relative error of at most 0.0077.
Values may be sent and summed in bfloat16 or wider, within the bound.
No kernel may reach another device: no remote copies, remote signals or barrier semaphores. Data moves between devices by JAX's collectives and lax.ppermute only.
A program may use at most 128 MiB of HBM per device.

v0:
```python
import jax
import jax.numpy as jnp
from jax import lax
from jax.sharding import PartitionSpec as P

mx_block = 32


def partner(x, axis, distance):
    return lax.ppermute(x, axis, [(i, i ^ 1 << distance) for i in range(lax.axis_size(axis))])


def dequantize(elems, scales, axis):
    return elems * jnp.repeat(scales, mx_block, axis=axis)


def rms_normed(rows, norm_gain):
    values = rows.astype(jnp.float32)
    factor = lax.rsqrt(jnp.mean(values * values, axis=-1, keepdims=True) + 1e-06)
    return (values * factor * norm_gain).astype(jnp.bfloat16)


def expert_hidden(rows, gate_up):
    both = jnp.einsum("rd,gdf->grf", rows, gate_up, preferred_element_type=jnp.float32)
    return (jax.nn.silu(both[0]) * both[1]).astype(jnp.bfloat16)


def on_device(
    tokens,
    norm_gain,
    route_ids,
    route_weights,
    rows_left,
    gate_up_elems,
    gate_up_scales,
    down_elems,
    down_scales,
    swap_pairs,
):
    slots = lax.axis_size("expert")
    half = slots // 2
    steps, rows, width = tokens.shape
    top = route_ids.shape[2]
    cap = max(2, min(rows, 2 * rows * top // slots))
    here = lax.axis_index("expert")
    pair_iota = jnp.arange(half, dtype=jnp.int32)
    slot_iota = jnp.arange(slots, dtype=jnp.int32)
    own_flag = jnp.sum(jnp.where(pair_iota == here % half, swap_pairs, 0))
    initial = (gate_up_elems, gate_up_scales, down_elems, down_scales)
    swapped = initial
    results = []
    for step in range(steps):
        if step == steps // 2:
            received = partner(
                (gate_up_elems, gate_up_scales, down_elems, down_scales),
                "expert",
                slots.bit_length() - 2,
            )
            swapped = tuple(
                (jnp.where(own_flag > 0, other, mine) for mine, other in zip(initial, received))
            )
        ids = route_ids[step]
        normed = rms_normed(tokens[step], norm_gain)
        live = rows_left > step
        flat_live = jnp.repeat(live, top)
        flat_dest = ids.reshape(-1)
        hits = ((flat_dest[:, None] == slot_iota[None, :]) & flat_live[:, None]).astype(jnp.int32)
        rank = jnp.sum(jnp.cumsum(hits, axis=0) * hits, axis=1) - 1
        slot_index = jnp.where(flat_live, flat_dest * cap + rank, slots * cap)
        sources = jnp.repeat(normed, top, axis=0)
        send = (
            jnp.zeros((slots * cap, width), jnp.bfloat16)
            .at[slot_index]
            .set(sources, mode="drop")
            .reshape(slots, cap, width)
        )
        gate_up = dequantize(initial[0][0], initial[1][0], 1)
        down = dequantize(initial[2][0], initial[3][0], 0)
        arrived = lax.all_to_all(send, "expert", split_axis=0, concat_axis=0, tiled=True)
        piece = lax.all_gather(arrived, "dp", axis=0, tiled=True)
        flat = piece.reshape(-1, width)
        hidden = expert_hidden(flat, gate_up).reshape(piece.shape[0], piece.shape[1], -1)
        hidden_rows = hidden.reshape(-1, hidden.shape[2])
        summed = lax.psum_scatter(
            jnp.dot(hidden_rows, down, preferred_element_type=jnp.float32).astype(jnp.bfloat16),
            "dp",
            scatter_dimension=0,
            tiled=True,
        )
        result = summed.reshape(slots, cap, width)
        back = lax.all_to_all(result, "expert", split_axis=0, concat_axis=0, tiled=True)
        picked = back.reshape(-1, width)[jnp.minimum(slot_index, slots * cap - 1)]
        factor = route_weights[step].reshape(-1) * flat_live.astype(jnp.float32)
        mixed_step = jnp.sum(
            (picked.astype(jnp.float32) * factor[:, None]).reshape(rows, top, width), axis=1
        )
        results.append(mixed_step.astype(jnp.bfloat16))
    mixed = jnp.stack(results)
    return (mixed, swapped[0], swapped[1], swapped[2], swapped[3])


def solution(mesh):
    in_specs = (
        P(None, ("expert", "dp"), None),
        P(),
        P(None, ("expert", "dp"), None),
        P(None, ("expert", "dp"), None),
        P(("expert", "dp")),
        P("expert", None, None, "dp"),
        P("expert", None, None, "dp"),
        P("expert", "dp", None),
        P("expert", "dp", None),
        P(),
    )
    out_specs = (
        P(None, ("expert", "dp"), None),
        P("expert", None, None, "dp"),
        P("expert", None, None, "dp"),
        P("expert", "dp", None),
        P("expert", "dp", None),
    )
    return jax.shard_map(
        on_device, mesh=mesh, in_specs=in_specs, out_specs=out_specs, check_vma=False
    )
```

profile of v0, /device:TPU:0, one launch (start us, length us, event | category | flops | bytes accessed | tf_op | source)
XLA Modules:
  0.0 702.3 jit_solution(17926109491885856133)
XLA Ops:
  7.2 0.7 broadcast_compare_fusion.1
  7.8 0.1 broadcast_in_dim.20
  7.9 0.1 and.26
  8.0 0.1 reshape.274
  8.1 0.7 fusion.57
  8.8 0.1 eq.38
  8.9 0.1 fusion.43
  9.0 0.1 reduce_window_sum.17
  9.1 0.2 select_reduce_fusion.1
  9.3 0.1 mul.136
  9.4 1.0 fusion.36
  10.4 1.0 fusion.38
  11.4 2.4 scatter_custom_fusion
  13.8 8.3 %all-to-all-start = ((bf16[16,8,4096]{2,1,0:T(8,128)(2,1)}), bf16[16,8,4096]{2,1,0:T(8,128)(2,1)S(1)}, u32[]{:S(2)}, u32[]{:S(2)}) async-start(bf16[16,8,4096]{2,1,0:T(8,128)(2,1)} %bitcast.8), calls=%async_computation | async-start | bytes 2097152 | tf_op jit(solution)/shard_map/all_to_all | solution.py:79
  22.2 0.0 all-gather.3.cloned.1.call-start
  22.2 2.9 collective-permute-start.2
  25.1 0.1 broadcast_in_dim.44
  25.2 0.1 and.29
  25.3 0.1 reshape.281
  25.4 0.1 eq.42
  25.4 0.1 fusion.45
  25.5 0.1 reduce_window_sum.18
  25.6 0.1 mul.151
  25.7 0.2 select_reduce_fusion
  25.9 110.5 %all-to-all-done = bf16[16,8,4096]{2,1,0:T(8,128)(2,1)S(1)} async-done(((bf16[16,8,4096]{2,1,0:T(8,128)(2,1)}), bf16[16,8,4096]{2,1,0:T(8,128)(2,1)S(1)}, u32[]{:S(2)}, u32[]{:S(2)}) %all-to-all-start) | async-done | bytes 1048608 | tf_op jit(solution)/shard_map/all_to_all | solution.py:79
  136.5 1.0 copy-done.1
  137.5 2.4 scatter_custom_fusion.1
  139.9 7.3 %all-to-all-start.2 = ((bf16[16,8,4096]{2,1,0:T(8,128)(2,1)}), bf16[16,8,4096]{2,1,0:T(8,128)(2,1)S(1)}, u32[]{:S(2)}, u32[]{:S(2)}) async-start(bf16[16,8,4096]{2,1,0:T(8,128)(2,1)} %bitcast.27), calls=%async_computation.3 | async-start | bytes 2097152 | tf_op jit(solution)/shard_map/all_to_all | solution.py:79
  147.1 0.0 all-gather.5.cloned.1.call-start
  147.2 0.6 fusion.46
  148.5 100.4 %all-to-all-done.2 = bf16[16,8,4096]{2,1,0:T(8,128)(2,1)S(1)} async-done(((bf16[16,8,4096]{2,1,0:T(8,128)(2,1)}), bf16[16,8,4096]{2,1,0:T(8,128)(2,1)S(1)}, u32[]{:S(2)}, u32[]{:S(2)}) %all-to-all-start.2) | async-done | bytes 1048608 | tf_op jit(solution)/shard_map/all_to_all | solution.py:79
  248.9 1.0 copy-done.2
  249.9 0.0 reduce-scatter.3.cloned.1.call-start
  250.0 0.0 all-gather.3.cloned.1.call-done
  250.0 0.7 broadcast_in_dim.19
  250.8 0.9 copy-done.9
  251.6 8.4 %fusion.10 = f32[2,256,512]{1,2,0:T(8,128)S(1)} fusion(bf16[32,8,4096]{2,1,0:T(8,128)(2,1)S(1)} %copy-done.9, bf16[1,2,4096,512]{3,2,1,0:T(8,128)(2,1)} %param.15, bf16[1,2,4096,512]{3,2,1,0:T(8,128)(2,1)S(1)} %bitcast.100), kind=kOutput, calls=%fused_computation.19 | convolution fusion | flops 2151677952 | bytes 19922944 | tf_op jit(solution)/shard_map/rd,gdf->grf/dot_general | solution.py:24
  260.1 0.5 broadcast_in_dim.23
  260.6 1.7 copy-done.3
  262.2 2.5 broadcast_select_fusion.1
  264.7 2.0 copy-done.4
  266.7 2.7 convolution_convert_fusion.1
  269.4 0.2 reduce-scatter.5.cloned.1.call-start
  269.6 2.7 collective-permute-start
  272.3 9.7 %fusion.15 = f32[2,256,512]{1,2,0:T(8,128)S(1)} fusion(bf16[32,8,4096]{2,1,0:T(8,128)(2,1)} %all-gather.5.cloned.1.call-done, bf16[1,2,4096,512]{3,2,1,0:T(8,128)(2,1)} %param.15, bf16[1,2,4096,512]{3,2,1,0:T(8,128)(2,1)} %bitcast.101), kind=kOutput, calls=%fused_computation.20 | convolution fusion | flops 2151677952 | bytes 19922944 | tf_op jit(solution)/shard_map/rd,gdf->grf/dot_general | solution.py:24
  282.1 2.7 convolution_convert_fusion
  284.8 0.0 reduce-scatter.3.cloned.1.call-done
  284.8 6.9 all-to-all-start.1
  291.7 2.8 collective-permute-start.1
  294.5 0.2 collective-permute-start.3
  294.7 0.1 bitcast_select_fusion.1
  294.8 1.1 reduce-scatter.5.cloned.1.call-done
  295.9 365.8 %all-to-all-done.1 = bf16[16,8,4096]{2,1,0:T(8,128)(2,1)S(1)} async-done(((bf16[16,8,4096]{2,1,0:T(8,128)(2,1)}), bf16[16,8,4096]{2,1,0:T(8,128)(2,1)S(1)}, u32[]{:S(2)}, u32[]{:S(2)}) %all-to-all-start.1) | async-done | bytes 1048608 | tf_op jit(solution)/shard_map/all_to_all | solution.py:91
  661.7 8.6 %all-to-all-start.3 = ((bf16[16,8,4096]{2,1,0:T(8,128)(2,1)}), bf16[16,8,4096]{2,1,0:T(8,128)(2,1)S(1)}, u32[]{:S(2)}, u32[]{:S(2)}) async-start(bf16[16,8,4096]{2,1,0:T(8,128)(2,1)} %bitcast.102), calls=%async_computation.5 | async-start | bytes 2097152 | tf_op jit(solution)/shard_map/all_to_all | solution.py:91
  670.3 1.0 collective-permute-done.3
  671.2 0.7 broadcast_select_fusion.3
  671.9 0.7 broadcast_select_fusion.2
  672.7 7.3 %broadcast_select_fusion = bf16[1,2,4096,512]{3,2,1,0:T(8,128)(2,1)} fusion(bf16[1,2,4096,512]{3,2,1,0:T(8,128)(2,1)} %collective-permute-done, bf16[1,2,4096,512]{3,2,1,0:T(8,128)(2,1)} %param.15, pred[]{:T(512)S(6)} %gt.14), kind=kLoop, calls=%fused_computation.8 | loop fusion | flops 4194304 | bytes 25165824 | tf_op jit(solution)/shard_map/jit(_where)/select_n | solution.py:60
  679.9 0.9 gather_fusion
  680.8 0.5 fusion.21
  681.2 12.5 %all-to-all-done.3 = bf16[16,8,4096]{2,1,0:T(8,128)(2,1)S(1)} async-done(((bf16[16,8,4096]{2,1,0:T(8,128)(2,1)}), bf16[16,8,4096]{2,1,0:T(8,128)(2,1)S(1)}, u32[]{:S(2)}, u32[]{:S(2)}) %all-to-all-start.3) | async-done | bytes 1048608 | tf_op jit(solution)/shard_map/all_to_all | solution.py:91
  693.7 0.9 gather_fusion.1
  694.6 0.5 fusion.20
  695.1 0.7 pad_maximum_fusion
  (32 shorter events, 0.2 us)
Async XLA Ops:
  7.2 140.0 %copy-start.10 = (s32[8]{0:T(128)S(1)}, s32[8]{0:T(128)}, u32[]{:S(2)}) copy-start(s32[8]{0:T(128)} %param.19) | copy-start | bytes 100
  11.4 238.6 %copy-start.6 = (bf16[1,2,128,512]{3,2,1,0:T(8,128)(2,1)S(1)}, bf16[1,2,128,512]{3,2,1,0:T(8,128)(2,1)}, u32[]{:S(2)}) copy-start(bf16[1,2,128,512]{3,2,1,0:T(8,128)(2,1)} %param.16) | copy-start | bytes 786436
  13.8 122.6 %all-to-all-start = ((bf16[16,8,4096]{2,1,0:T(8,128)(2,1)}), bf16[16,8,4096]{2,1,0:T(8,128)(2,1)S(1)}, u32[]{:S(2)}, u32[]{:S(2)}) async-start(bf16[16,8,4096]{2,1,0:T(8,128)(2,1)} %bitcast.8), calls=%async_computation | async-start | bytes 2097152 | tf_op jit(solution)/shard_map/all_to_all | solution.py:79
  22.2 227.8 %all-gather.3.cloned.1.call-start = ((), (), s32[]{:S(2)}) async-start(), calls=%async_computation.6 | async-start | bytes 3145728 | tf_op jit(solution)/shard_map/all_gather | solution.py:80
  22.2 237.8 %collective-permute-start.2 = (bf16[1,512,4096]{2,1,0:T(8,128)(2,1)}, bf16[1,512,4096]{2,1,0:T(8,128)(2,1)}, u32[]{:S(2)}, u32[]{:S(2)}) collective-permute-start(bf16[1,512,4096]{2,1,0:T(8,128)(2,1)} %param.17), channel_id=1, source_target_pairs={{0,16},{2,18},{4,20},{6,22},{8,24},{10,26},{12,28},{14,30},{16,0},... | collective-permute-start | bytes 12582920 | tf_op jit(solution)/shard_map/ppermute | solution.py:10
  136.5 1.0 copy-start.1
  139.9 109.1 %all-to-all-start.2 = ((bf16[16,8,4096]{2,1,0:T(8,128)(2,1)}), bf16[16,8,4096]{2,1,0:T(8,128)(2,1)S(1)}, u32[]{:S(2)}, u32[]{:S(2)}) async-start(bf16[16,8,4096]{2,1,0:T(8,128)(2,1)} %bitcast.27), calls=%async_computation.3 | async-start | bytes 2097152 | tf_op jit(solution)/shard_map/all_to_all | solution.py:79
  147.1 125.1 %all-gather.5.cloned.1.call-start = ((), (), s32[]{:S(2)}) async-start(), calls=%async_computation.8 | async-start | bytes 3145728 | tf_op jit(solution)/shard_map/all_gather | solution.py:80
  248.9 1.0 copy-start.2
  249.9 34.9 %reduce-scatter.3.cloned.1.call-start = ((), (), s32[]{:S(2)}) async-start(), calls=%async_computation.7 | async-start | bytes 3145728 | tf_op jit(solution)/shard_map/reduce_scatter | solution.py:84
  250.0 1.6 copy-start.9
  250.7 9.3 %copy-start = (bf16[2,128,32,512]{3,2,1,0:T(8,128)(2,1)}, bf16[2,128,32,512]{3,2,1,0:T(8,128)(2,1)S(1)}, u32[]{:S(2)}) copy-start(bf16[2,128,32,512]{3,2,1,0:T(8,128)(2,1)S(1)} %broadcast_in_dim.19) | copy-start | bytes 25165828
  251.6 8.4 %copy-start.7 = (bf16[1,16,4096]{2,1,0:T(8,128)(2,1)S(1)}, bf16[1,16,4096]{2,1,0:T(8,128)(2,1)}, u32[]{:S(2)}) copy-start(bf16[1,16,4096]{2,1,0:T(8,128)(2,1)} %param.18) | copy-start | bytes 393220
  260.0 2.2 copy-start.3
  264.7 2.0 copy-start.4
  269.4 26.5 %reduce-scatter.5.cloned.1.call-start = ((), (), s32[]{:S(2)}) async-start(), calls=%async_computation.9 | async-start | bytes 3145728 | tf_op jit(solution)/shard_map/reduce_scatter | solution.py:84
  269.6 403.1 %collective-permute-start = (bf16[1,2,4096,512]{3,2,1,0:T(8,128)(2,1)}, bf16[1,2,4096,512]{3,2,1,0:T(8,128)(2,1)}, u32[]{:S(2)}, u32[]{:S(2)}) collective-permute-start(bf16[1,2,4096,512]{3,2,1,0:T(8,128)(2,1)} %param.15), channel_id=1, source_target_pairs={{0,16},{2,18},{4,20},{6,22},{8,24},{10,26},{12,28},{14,30},{16,0},... | collective-permute-start | bytes 25165832 | tf_op jit(solution)/shard_map/ppermute | solution.py:10
  272.3 9.7 %copy-start.5 = (bf16[1,512,4096]{2,1,0:T(8,128)(2,1)S(1)}, bf16[1,512,4096]{2,1,0:T(8,128)(2,1)}, u32[]{:S(2)}) copy-start(bf16[1,512,4096]{2,1,0:T(8,128)(2,1)} %copy-done.4) | copy-start | bytes 12582916
  282.0 12.6 %copy-start.8 = (f32[2,8,8]{2,1,0:T(8,128)S(1)}, f32[2,8,8]{2,1,0:T(8,128)}, u32[]{:S(2)}) copy-start(f32[2,8,8]{2,1,0:T(8,128)} %param.13) | copy-start | bytes 1540
  284.8 376.9 %all-to-all-start.1 = ((bf16[16,8,4096]{2,1,0:T(8,128)(2,1)}), bf16[16,8,4096]{2,1,0:T(8,128)(2,1)S(1)}, u32[]{:S(2)}, u32[]{:S(2)}) async-start(bf16[16,8,4096]{2,1,0:T(8,128)(2,1)} %bitcast.103), calls=%async_computation.2 | async-start | bytes 2097152 | tf_op jit(solution)/shard_map/all_to_all | solution.py:91
  291.7 380.3 %collective-permute-start.1 = (bf16[1,2,128,512]{3,2,1,0:T(8,128)(2,1)S(1)}, bf16[1,2,128,512]{3,2,1,0:T(8,128)(2,1)S(1)}, u32[]{:S(2)}, u32[]{:S(2)}) collective-permute-start(bf16[1,2,128,512]{3,2,1,0:T(8,128)(2,1)S(1)} %copy-done.6), channel_id=1, source_target_pairs={{0,16},{2,18},{4,20},{6,22},{8,24},{10,26},{12,28},{14,30},{16,0},... | collective-permute-start | bytes 786440 | tf_op jit(solution)/shard_map/ppermute | solution.py:10
  294.5 376.8 %collective-permute-start.3 = (bf16[1,16,4096]{2,1,0:T(8,128)(2,1)S(1)}, bf16[1,16,4096]{2,1,0:T(8,128)(2,1)S(1)}, u32[]{:S(2)}, u32[]{:S(2)}) collective-permute-start(bf16[1,16,4096]{2,1,0:T(8,128)(2,1)S(1)} %copy-done.7), channel_id=1, source_target_pairs={{0,16},{2,18},{4,20},{6,22},{8,24},{10,26},{12,28},{14,30},{16,0},... | collective-permute-start | bytes 393224 | tf_op jit(solution)/shard_map/ppermute | solution.py:10
  661.7 32.1 %all-to-all-start.3 = ((bf16[16,8,4096]{2,1,0:T(8,128)(2,1)}), bf16[16,8,4096]{2,1,0:T(8,128)(2,1)S(1)}, u32[]{:S(2)}, u32[]{:S(2)}) async-start(bf16[16,8,4096]{2,1,0:T(8,128)(2,1)} %bitcast.102), calls=%async_computation.5 | async-start | bytes 2097152 | tf_op jit(solution)/shard_map/all_to_all | solution.py:91
Sparse Core Ops, SparseCore 0:
  137.6 12.2 all-gather.2
  250.1 10.7 all-gather.4
  269.5 11.4 reduce-scatter.2
  284.9 10.9 reduce-scatter.4
where the time goes:
time: 703 us; the launch traced here: 702 us
  waiting for transfers between devices  591 us (84%)
  starting transfers between devices  40 us (6%)
  matrix products  23.5 us (3%)
  other arithmetic  17.6 us (3%)
  local copies, waits for them, and re-layouts  15 us (2%)
  between operations  14.7 us (2%)
    all_to_all x2, waiting for transfers between devices, on_device(): lax.all_to_all(result, 'expert', split_axis=0, concat_axis=0, tiled=True)  378 us
    all_to_all x2, waiting for transfers between devices, on_device(): lax.all_to_all(send, 'expert', split_axis=0, concat_axis=0, tiled=True)  211 us
    dot_general x2, matrix products, expert_hidden(): jnp.einsum('rd,gdf->grf', rows, gate_up, preferred_element_type=jnp.float32)  18.1 us
    all_to_all x2, starting transfers between devices, on_device(): lax.all_to_all(send, 'expert', split_axis=0, concat_axis=0, tiled=True)  15.6 us
    all_to_all x2, starting transfers between devices, on_device(): lax.all_to_all(result, 'expert', split_axis=0, concat_axis=0, tiled=True)  15.4 us
  transfers between devices with their start and end apart: 12, of which 6 were waited for; matrix products, arithmetic and copies ran while one was open for 6% of the time, Pallas kernels for 0%

commit v1 on v0

v1 whole, which is shorter than its diff:
```python
import jax
import jax.numpy as jnp
from jax import lax
from jax.experimental import pallas as pl
from jax.experimental.pallas import tpu as pltpu
from jax.sharding import PartitionSpec as P


mx_block = 32
columns = 4


def flip(x, axis, bit):
    return lax.ppermute(x, axis, [(i, i ^ 1 << bit) for i in range(lax.axis_size(axis))])


def dequantize(elems, scales, axis):
    return elems * jnp.repeat(scales, mx_block, axis=axis)


def rms_normed(rows, norm_gain):
    values = rows.astype(jnp.float32)
    factor = lax.rsqrt(jnp.mean(values * values, axis=-1, keepdims=True) + 1e-06)
    return (values * factor * norm_gain).astype(jnp.bfloat16)


def expert_hidden(rows, gate_up):
    both = jnp.einsum("rd,gdf->grf", rows, gate_up, preferred_element_type=jnp.float32)
    return (jax.nn.silu(both[0]) * both[1]).astype(jnp.bfloat16)


def hops(x, axis, low, radix, pick=lambda x, d: x):
    n = lax.axis_size(axis)
    got = []
    for d in range(1, radix):
        got.append(lax.ppermute(pick(x, d), axis, [(i, i ^ d << low) for i in range(n)]))
    return got


def stages():
    bits = lax.axis_size("expert").bit_length() - 1
    order = [("expert", b - 2, 4) for b in range(bits, 1, -2)]
    if bits % 2:
        order = [("expert", 0, 2)] + [("expert", b - 2, 4) for b in range(bits, 2, -2)]
    low = 0
    size = lax.axis_size("dp")
    while size > 1:
        order.append(("dp", low, 2))
        low, size = low + 1, size // 2
    return order


def after(x, *others):
    return lax.optimization_barrier((x, *others))


def total(xs):
    out = xs[0].astype(jnp.float32)
    for x in xs[1:]:
        out = out + x.astype(jnp.float32)
    return out.astype(jnp.bfloat16)


def sender(tokens, norm_gain, route_ids, route_weights, rows_left):
    steps, rows, width = tokens.shape
    slots = lax.axis_size("expert")
    normed = rms_normed(tokens, norm_gain).reshape(steps * rows, width)
    live = (rows_left[None, :] > jnp.arange(steps)[:, None]).astype(jnp.float32)
    hits = route_ids[..., None] == jnp.arange(slots, dtype=jnp.int32)
    share = jnp.sum(jnp.where(hits, (route_weights * live[..., None])[..., None], 0.0), axis=2)
    share = share.reshape(steps * rows, slots)
    parts = []
    for _ in range(3):
        part = lax.reduce_precision(share, 8, 7)
        parts.append(part.astype(jnp.bfloat16))
        share = share - part
    parts = jnp.concatenate(parts, axis=1)
    parts = jnp.pad(parts, ((0, 0), (0, -parts.shape[1] % 128)))
    return jnp.concatenate([parts, normed], axis=1), parts.shape[1]


def expert_rows(everything, side, weights):
    gate_up_elems, gate_up_scales, down_elems, down_scales = weights
    slots = lax.axis_size("expert")
    here = lax.axis_index("expert")
    column = jnp.arange(side, dtype=jnp.int32)
    mine = (column % slots == here) & (column < 3 * slots)
    factor = jnp.sum(
        jnp.where(mine, everything[:, :side].astype(jnp.float32), 0.0), axis=1, keepdims=True
    )
    hidden = expert_hidden(
        everything[:, side:], dequantize(gate_up_elems[0], gate_up_scales[0], 1)
    )
    out = jnp.dot(
        hidden, dequantize(down_elems[0], down_scales[0], 0), preferred_element_type=jnp.float32
    )
    return (out * factor).astype(jnp.bfloat16)


def gather_stage(block, stage):
    return jnp.concatenate([block, *hops(block, *stage)])


def scatter_stage(block, stage):
    n = block.shape[0] // stage[2]
    others = hops(block, *stage, pick=lambda x, d: x[d * n : (d + 1) * n])
    return total([block[:n], *others])


eighths = (0, 1, 3, 4, 5, 6, 8)


def row_map(down_shape, down_s_rows, gate_up_s_rows, gate_up_rows, hidden):
    rows, width = down_shape
    blocks = width // hidden
    first = blocks * 5 // 8
    entries = [(0, b * rows, 2, 0, b * hidden, rows) for b in range(first)]
    runs = [(2, 0, b * hidden, rows) for b in range(first, blocks)]
    runs += [(3, 0, b * hidden, down_s_rows) for b in range(blocks)]
    runs += [(1, 0, 0, gate_up_s_rows), (0, 0, 0, gate_up_rows)]
    length = sum(run[3] for run in runs)
    cuts = [length * e // 64 * 8 for e in eighths]
    cuts[-1] = length
    at = 0
    for array, row, column, count in runs:
        while count:
            k = max(j for j in range(len(cuts) - 1) if cuts[j] <= at)
            size = min(count, cuts[k + 1] - at)
            entries.append((k + 1, at - cuts[k], array, row, column, size))
            at, row, count = at + size, row + size, count - size
    heights = [first * rows] + [b - a for a, b in zip(cuts, cuts[1:])]
    return heights, entries


def copies(moves, buffer, in_sems, out_sems):
    at, arriving, leaving = 0, [], []
    for k, (src, dst) in enumerate(moves):
        rows = buffer.at[pl.ds(at, src.shape[0]), :]
        at += src.shape[0]
        arriving.append(pltpu.make_async_copy(src, rows, in_sems.at[k]))
        leaving.append(pltpu.make_async_copy(rows, dst, out_sems.at[k]))
    for copy in arriving:
        copy.start()
    for into, out in zip(arriving, leaving):
        into.wait()
        out.start()
    for copy in leaving:
        copy.wait()


def staging(entries, hidden):
    return [
        pltpu.VMEM((sum(entry[-1] for entry in entries), hidden), jnp.bfloat16),
        pltpu.SemaphoreType.DMA((len(entries),)),
        pltpu.SemaphoreType.DMA((len(entries),)),
    ]


def gather_blocks(arrays, heights, entries, hidden):
    def body(*refs):
        ins, outs, scratch = refs[:4], refs[4:-3], refs[-3:]
        copies(
            [
                (
                    ins[a].at[pl.ds(row, n), pl.ds(column, hidden)],
                    outs[block].at[pl.ds(at, n), :],
                )
                for block, at, a, row, column, n in entries
            ],
            *scratch,
        )

    hbm = pl.BlockSpec(memory_space=pl.ANY)
    return pl.pallas_call(
        body,
        out_shape=[jax.ShapeDtypeStruct((h, hidden), jnp.bfloat16) for h in heights],
        in_specs=[hbm] * 4,
        out_specs=[hbm] * len(heights),
        scratch_shapes=staging(entries, hidden),
        name="gather_blocks",
    )(*arrays)


def place_blocks(choice, arrays, early, received, entries, hidden):
    planes, count = len(received), len(received[0])

    def body(choice_ref, *refs):
        own, first, refs = refs[:4], refs[4], refs[5:]
        segments = [refs[p * count : (p + 1) * count] for p in range(planes)]
        outs, scratch = refs[planes * count : -3], refs[-3:]

        def rectangle(arrays, entry):
            _, _, a, row, column, n = entry
            return arrays[a].at[pl.ds(row, n), pl.ds(column, hidden)]

        @pl.when(choice_ref[0] == 0)
        def _():
            copies([(rectangle(own, e), rectangle(outs, e)) for e in entries], *scratch)

        for p in range(planes):

            @pl.when(choice_ref[0] == p + 1)
            def _():
                blocks = [first, *segments[p]]
                copies(
                    [(blocks[e[0]].at[pl.ds(e[1], e[-1]), :], rectangle(outs, e)) for e in entries],
                    *scratch,
                )

    hbm = pl.BlockSpec(memory_space=pl.ANY)
    flat = [x for got in received for x in got]
    return pl.pallas_call(
        body,
        out_shape=[jax.ShapeDtypeStruct(x.shape, x.dtype) for x in arrays],
        in_specs=[pl.BlockSpec(memory_space=pltpu.SMEM)] + [hbm] * (5 + len(flat)),
        out_specs=[hbm] * 4,
        scratch_shapes=staging(entries, hidden),
        name="place_blocks",
    )(choice, *arrays, early, *flat)


def moved_pairs(mask, plane, half, own, held):
    active = [c for c in range(columns) if mask >> c & 1]
    if not active:
        return tuple(jnp.zeros_like(x) for x in own)

    def send(x, pairs):
        pairs = [
            (s * half + plane * columns + a, (1 - s) * half + plane * columns + b)
            for a, b in pairs
            for s in (0, 1)
        ]
        return lax.ppermute(x, "expert", pairs)

    direct = [(c, c) for c in active]
    if len(active) == 4:
        return tuple(send(x, direct) for x in own)
    if len(active) == 1:
        c = active[0]
        x = [send(held[k], [(c ^ 1, c)]) for k in (0, 1)]
        y = [send(held[k], [(c ^ 2, c)]) for k in (4, 5)]
        return (*x, send(own[2], direct), send(own[3], direct), *y)
    if len(active) == 2:
        a, b = active
        d = 2 if a ^ b == 1 else 1
        helped = (3, 4, 5) if d == 2 else (0, 1, 2)
        return tuple(
            send(held[k], [(a ^ d, a), (b ^ d, b)]) if k in helped else send(own[k], direct)
            for k in range(6)
        )
    h = (set(range(columns)) - set(active)).pop()
    a, b, d = h ^ 1, h ^ 2, h ^ 3
    me = lax.axis_index("expert") % columns
    front = [
        send(jnp.where(me == h, held[k], own[k]), [(h, a), (b, b), (d, d)]) for k in (0, 1, 2)
    ]
    back = send(held[5], [(h, b), (a, d)])
    own_back = send(own[5], [(a, a)])
    return (*front, send(own[3], direct), send(own[4], direct), jnp.where(me == a, own_back, back))


def on_device(
    tokens,
    norm_gain,
    route_ids,
    route_weights,
    rows_left,
    gate_up_elems,
    gate_up_scales,
    down_elems,
    down_scales,
    swap_pairs,
):
    weights = (gate_up_elems, gate_up_scales, down_elems, down_scales)
    slots = lax.axis_size("expert")
    half = slots // 2
    top_bit = slots.bit_length() - 2
    pair = lax.axis_index("expert") % half
    flag = jnp.sum(jnp.where(jnp.arange(half, dtype=jnp.int32) == pair, swap_pairs, 0)) > 0
    block, side = sender(tokens, norm_gain, route_ids, route_weights, rows_left)
    order = stages()
    planes = half // columns
    if planes != 2:
        received = flip(weights, "expert", top_bit)
        for stage in order:
            block = gather_stage(block, stage)
        block = expert_rows(block, side, weights)
        for stage in reversed(order):
            block = scatter_stage(block, stage)
        new = tuple((jnp.where(flag, other, mine) for mine, other in zip(weights, received)))
        return (block.reshape(tokens.shape), *new)

    hidden = gate_up_elems.shape[3]
    flat = (
        gate_up_elems.reshape(-1, hidden),
        gate_up_scales.reshape(-1, hidden),
        down_elems[0],
        down_scales[0],
    )
    heights, entries = row_map(
        flat[2].shape, flat[3].shape[0], flat[1].shape[0], flat[0].shape[0], hidden
    )
    early, *own = gather_blocks(flat, heights, entries, hidden)
    held = [None] * 6

    def spread(ks, *tied):
        tied, given = tied[0], [own[k] for k in ks]
        if tied is not None:
            tied, *given = after(tied, *given)
        for k, x in zip(ks, given):
            held[k] = flip(x, "expert", 0 if k < 3 else 1)
        return tied

    z_stage, plane_stage, dp_stages = order[0], order[1], order[2:]
    spread((0, 3), None)
    block = gather_stage(block, z_stage)
    block, early = after(block, early)
    early = flip(early, "expert", top_bit)
    block = gather_stage(block, plane_stage)
    block = spread((1, 5), block)
    for stage in dp_stages:
        block = gather_stage(block, stage)
    block = expert_rows(block, side, weights)
    for stage in reversed(dp_stages):
        block = scatter_stage(block, stage)
    block = scatter_stage(block, plane_stage)
    block = spread((2, 4), block)
    block = scatter_stage(block, z_stage)
    mixed, swap_pairs, early, *held = after(block, swap_pairs, early, *held)
    received = []
    for plane in range(planes):
        bits = swap_pairs[plane * columns : (plane + 1) * columns]
        mask = jnp.sum(jnp.where(bits > 0, 1 << jnp.arange(columns, dtype=jnp.int32), 0))
        got = lax.switch(
            mask,
            [
                (lambda m: lambda own, held: moved_pairs(m, plane, half, own, held))(m)
                for m in range(1 << columns)
            ],
            tuple(own),
            tuple(held),
        )
        received.append(got)
    choice = jnp.where(flag, 1 + pair // columns, 0).astype(jnp.int32).reshape(1)
    new = place_blocks(choice, flat, early, received, entries, hidden)
    return (
        mixed.reshape(tokens.shape),
        *(x.reshape(old.shape) for x, old in zip(new, weights)),
    )


def solution(mesh):
    in_specs = (
        P(None, ("expert", "dp"), None),
        P(),
        P(None, ("expert", "dp"), None),
        P(None, ("expert", "dp"), None),
        P(("expert", "dp")),
        P("expert", None, None, "dp"),
        P("expert", None, None, "dp"),
        P("expert", "dp", None),
        P("expert", "dp", None),
        P(),
    )
    out_specs = (
        P(None, ("expert", "dp"), None),
        P("expert", None, None, "dp"),
        P("expert", None, None, "dp"),
        P("expert", "dp", None),
        P("expert", "dp", None),
    )

    return jax.shard_map(
        on_device, mesh=mesh, in_specs=in_specs, out_specs=out_specs, check_vma=False
    )
```

time: 703 us -> 681 us (0.969)
  the two profiles are of different devices: /device:TPU:0 before, /device:TPU:12 now
where the time goes in v1:
time: 681 us; the launch traced here: 672 us
  starting transfers between devices  308 us (45%)
  waiting for transfers between devices  300 us (44%)
  other arithmetic  26 us (4%)
  Pallas kernels  19.7 us (3%)
  local copies, waits for them, and re-layouts  7.62 us (1%)
  matrix products  7.12 us (1%)
    ppermute x13, starting transfers between devices, send(): return lax.ppermute(x, 'expert', pairs)  251 us
    ppermute x13, waiting for transfers between devices, send(): return lax.ppermute(x, 'expert', pairs)  136 us
    ppermute x14, waiting for transfers between devices, hops(): lax.ppermute(pick(x, d), axis, [(i, i ^ d << low) for i in range(n)])  126 us
    ppermute x7, starting transfers between devices, flip(): lax.ppermute(x, axis, [(i, i ^ 1 << bit) for i in range(lax.axis_size(axi...  41.3 us
    ppermute x7, waiting for transfers between devices, flip(): lax.ppermute(x, axis, [(i, i ^ 1 << bit) for i in range(lax.axis_size(axi...  37.9 us
    ppermute x14, starting transfers between devices, hops(): lax.ppermute(pick(x, d), axis, [(i, i ^ d << low) for i in range(n)])  16.1 us
  transfers between devices with their start and end apart: 34, of which 13 were waited for; matrix products, arithmetic and copies ran while one was open for 3% of the time, Pallas kernels for 1%

profile of v1, /device:TPU:12, one launch (start us, length us, event | category | flops | bytes accessed | tf_op | source)
XLA Modules:
  0.0 672.4 jit_solution(4668138626824406326)
XLA Ops:
  0.6 1.0 fusion.6
  2.3 0.8 broadcast_multiply_fusion
  3.1 0.8 select_reduce_fusion.1
  3.9 1.0 fusion.9
  5.0 1.6 collective-permute-start.190
  6.7 1.2 collective-permute-start.189
  7.9 1.2 collective-permute-start.188
  9.2 9.4 %gather_blocks.1 = (bf16[2560,512]{1,0:T(8,128)(2,1)}, bf16[1264,512]{1,0:T(8,128)(2,1)}, bf16[2528,512]{1,0:T(8,128)(2,1)S(1)}, bf16[1264,512]{1,0:T(8,128)(2,1...) custom-call(bf16[8192,512]{1,0:T(8,128)(2,1)} %bitcast.41, ...), custom_call_target="tpu_custom_call" | custom-call | tf_op jit(solution)/shard_map/gather_blocks/pallas_call | solution.py:174
  18.6 1.5 collective-permute-start.193
  20.1 1.5 collective-permute-start.192
  22.2 12.6 %collective-permute-done.193 = bf16[64,4224]{1,0:T(8,128)(2,1)S(1)} collective-permute-done((bf16[64,4224]{1,0:T(8,128)(2,1)S(1)}, bf16[64,4224]{1,0:T(8,128)(2,1)S(1)}, u32[]{:S(2)}, u32[]{:S(2)}) %collective-permute-start.193) | collective-permute-done | bytes 540704 | tf_op jit(solution)/shard_map/ppermute | solution.py:36
  34.8 9.8 %collective-permute-done.192 = bf16[64,4224]{1,0:T(8,128)(2,1)S(1)} collective-permute-done((bf16[64,4224]{1,0:T(8,128)(2,1)S(1)}, bf16[64,4224]{1,0:T(8,128)(2,1)S(1)}, u32[]{:S(2)}, u32[]{:S(2)}) %collective-permute-start.192) | collective-permute-done | bytes 540704 | tf_op jit(solution)/shard_map/ppermute | solution.py:36
  44.6 1.5 pad_maximum_fusion
  46.2 7.4 %bitcast_multiply_fusion = bf16[2,4096,512]{2,1,0:T(8,128)(2,1)} fusion(bf16[1,2,4096,512]{3,2,1,0:T(8,128)(2,1)} %param.47, bf16[2,128,512]{2,1,0:T(8,128)(2,1)S(1)} %bitcast.50), kind=kLoop, calls=%fused_computation.32 | loop fusion | flops 4194304 | bytes 17039360 | tf_op jit(solution)/shard_map/mul | solution.py:18
  54.1 1.7 copy-done.18
  55.8 2.6 bitcast_multiply_fusion.1
  58.4 2.2 constant_dynamic-update-slice_fusion.1
  60.5 1.9 constant_dynamic-update-slice_fusion
  62.6 4.6 fusion.2
  67.2 2.6 multiply_convert_fusion
  70.5 3.8 collective-permute-done.195
  74.2 0.8 add_convert_fusion
  75.2 1.6 collective-permute-start.198
  76.8 0.7 collective-permute-start.197
  77.5 1.2 collective-permute-start.196
  78.7 5.3 collective-permute-start.203
  84.0 16.7 %collective-permute-start.206 = (bf16[1264,512]{1,0:T(8,128)(2,1)}, bf16[1264,512]{1,0:T(8,128)(2,1)S(1)}, u32[]{:S(2)}, u32[]{:S(2)}) collective-permute-start(bf16[1264,512]{1,0:T(8,128)(2,1)} %get-tuple-element.693), channel_id=1, source_target_pairs={{0,4},{2,6},{4,0},{6,2},{8,12},{10,14},{12,8},{14,10},{16,20},{18,... | collective-permute-start | bytes 3883016 | tf_op jit(solution)/shard_map/ppermute | solution.py:14
  100.8 5.8 collective-permute-start.202
  106.6 5.7 collective-permute-start.204
  112.3 5.7 collective-permute-start.208
  118.3 10.7 %collective-permute-done.203 = bf16[1264,512]{1,0:T(8,128)(2,1)S(1)} collective-permute-done((bf16[1264,512]{1,0:T(8,128)(2,1)S(1)}, bf16[1264,512]{1,0:T(8,128)(2,1)S(1)}, u32[]{:S(2)}, u32[]{:S(2)}) %collective-permute-start.203) | collective-permute-done | bytes 1294368 | tf_op jit(solution)/shard_map/ppermute | solution.py:14
  129.1 1.0 copy-done.9
  130.1 1.4 collective-permute-start.201
  131.6 2.8 collective-permute-start.200
  134.4 96.2 %collective-permute-done.201 = bf16[16,4096]{1,0:T(8,128)(2,1)S(1)} collective-permute-done((bf16[16,4096]{1,0:T(8,128)(2,1)S(1)}, bf16[16,4096]{1,0:T(8,128)(2,1)S(1)}, u32[]{:S(2)}, u32[]{:S(2)}) %collective-permute-start.201) | collective-permute-done | bytes 131104 | tf_op jit(solution)/shard_map/ppermute | solution.py:36
  230.9 1.5 collective-permute-start.205
  232.4 3.2 collective-permute-done.199
  237.4 0.7 add_convert_fusion.2
  238.2 23.4 %collective-permute-done.205 = bf16[1264,512]{1,0:T(8,128)(2,1)} collective-permute-done((bf16[1264,512]{1,0:T(8,128)(2,1)}, bf16[1264,512]{1,0:T(8,128)(2,1)}, u32[]{:S(2)}, u32[]{:S(2)}) %collective-permute-start.205) | collective-permute-done | bytes 1294368 | tf_op jit(solution)/shard_map/ppermute | solution.py:14
  261.6 3.7 collective-permute-done.207
  265.3 0.7 fusion.19
  267.3 22.9 %conditional.2 = (bf16[1264,512]{1,0:T(8,128)(2,1)}, bf16[2528,512]{1,0:T(8,128)(2,1)}, bf16[1264,512]{1,0:T(8,128)(2,1)}, bf16[1264,512]{1,0:T(8,128)(2,1)}, bf...) conditional(s32[]{:T(128)} %clamp.6, () %tuple.144, ...), branch_computations={%region_5.6_spmd, %region_6.7_spmd, %region_7.8_spmd, %region_8.9_... | conditional | flops 3883024 | bytes 85426720 | solution.py:334
  267.3 7.5 %collective-permute-start.18 = (bf16[1264,512]{1,0:T(8,128)(2,1)}, bf16[1264,512]{1,0:T(8,128)(2,1)}, u32[]{:S(2)}, u32[]{:S(2)}) collective-permute-start(bf16[1264,512]{1,0:T(8,128)(2,1)} %get-tuple-element.442), channel_id=1, source_target_pairs={{6,20},{22,4},{7,21},{23,5}} | collective-permute-start | bytes 3883016 | tf_op jit(solution)/shard_map/cond/branch_4_fun/ppermute | solution.py:233
  274.8 7.9 %collective-permute-start.19 = (bf16[2528,512]{1,0:T(8,128)(2,1)}, bf16[2528,512]{1,0:T(8,128)(2,1)}, u32[]{:S(2)}, u32[]{:S(2)}) collective-permute-start(bf16[2528,512]{1,0:T(8,128)(2,1)} %get-tuple-element.443), channel_id=1, source_target_pairs={{6,20},{22,4},{7,21},{23,5}} | collective-permute-start | bytes 7766024 | tf_op jit(solution)/shard_map/cond/branch_4_fun/ppermute | solution.py:233
  282.7 2.1 collective-permute-start.23
  284.9 1.7 collective-permute-start.20
  286.6 1.7 collective-permute-start.21
  288.3 1.7 collective-permute-start.22
  290.2 371.4 %conditional.3 = (bf16[1264,512]{1,0:T(8,128)(2,1)}, bf16[2528,512]{1,0:T(8,128)(2,1)}, bf16[1264,512]{1,0:T(8,128)(2,1)}, bf16[1264,512]{1,0:T(8,128)(2,1)}, bf...) conditional(s32[]{:T(128)} %clamp.7, () %tuple.150, ...), branch_computations={%region_22.23_spmd, %region_23.24_spmd, %region_24.25_spmd, %regio... | conditional | flops 3883024 | bytes 85426720 | solution.py:334
  290.3 2.2 collective-permute-start.179
  292.5 1.3 collective-permute-start.180
  293.8 1.8 broadcast_select_fusion.25
  295.5 195.9 %collective-permute-start.175 = (bf16[2528,512]{1,0:T(8,128)(2,1)}, bf16[2528,512]{1,0:T(8,128)(2,1)}, u32[]{:S(2)}, u32[]{:S(2)}) collective-permute-start(bf16[2528,512]{1,0:T(8,128)(2,1)} %broadcast_select_fusion.25), channel_id=1, source_target_pairs={{10,24},{26,8},{14,30},{30,14},{12,28},{28,12},{11,25},{27,9},{15,... | collective-permute-start | bytes 7766024 | tf_op jit(solution)/shard_map/cond/branch_13_fun/ppermute | solution.py:233
  491.6 7.5 %collective-permute-start.174 = (bf16[1264,512]{1,0:T(8,128)(2,1)S(1)}, bf16[1264,512]{1,0:T(8,128)(2,1)}, u32[]{:S(2)}, u32[]{:S(2)}) collective-permute-start(bf16[1264,512]{1,0:T(8,128)(2,1)S(1)} %broadcast_select_fusion.27), channel_id=1, source_target_pairs={{10,24},{26,8},{14,30},{30,14},{12,28},{28,12},{11,25},{27,9},{15,... | collective-permute-start | bytes 3883016 | tf_op jit(solution)/shard_map/cond/branch_13_fun/ppermute | solution.py:233
  499.2 1.5 broadcast_select_fusion.26
  500.6 7.1 %collective-permute-start.176 = (bf16[1264,512]{1,0:T(8,128)(2,1)S(1)}, bf16[1264,512]{1,0:T(8,128)(2,1)}, u32[]{:S(2)}, u32[]{:S(2)}) collective-permute-start(bf16[1264,512]{1,0:T(8,128)(2,1)S(1)} %broadcast_select_fusion.26), channel_id=1, source_target_pairs={{10,24},{26,8},{14,30},{30,14},{12,28},{28,12},{11,25},{27,9},{15,... | collective-permute-start | bytes 3883016 | tf_op jit(solution)/shard_map/cond/branch_13_fun/ppermute | solution.py:233
  507.8 7.1 %collective-permute-start.177 = (bf16[1264,512]{1,0:T(8,128)(2,1)}, bf16[1264,512]{1,0:T(8,128)(2,1)}, u32[]{:S(2)}, u32[]{:S(2)}) collective-permute-start(bf16[1264,512]{1,0:T(8,128)(2,1)} %get-tuple-element.616), channel_id=1, source_target_pairs={{8,24},{24,8},{12,28},{28,12},{14,30},{30,14},{9,25},{25,9},{13,29... | collective-permute-start | bytes 3883016 | tf_op jit(solution)/shard_map/cond/branch_13_fun/ppermute | solution.py:233
  514.9 7.0 %collective-permute-start.178 = (bf16[1264,512]{1,0:T(8,128)(2,1)}, bf16[1264,512]{1,0:T(8,128)(2,1)}, u32[]{:S(2)}, u32[]{:S(2)}) collective-permute-start(bf16[1264,512]{1,0:T(8,128)(2,1)} %get-tuple-element.617), channel_id=1, source_target_pairs={{8,24},{24,8},{12,28},{28,12},{14,30},{30,14},{9,25},{25,9},{13,29... | collective-permute-start | bytes 3883016 | tf_op jit(solution)/shard_map/cond/branch_13_fun/ppermute | solution.py:233
  521.9 3.5 broadcast_select_fusion.24
  525.4 53.5 %collective-permute-done.174 = bf16[1264,512]{1,0:T(8,128)(2,1)} collective-permute-done((bf16[1264,512]{1,0:T(8,128)(2,1)S(1)}, bf16[1264,512]{1,0:T(8,128)(2,1)}, u32[]{:S(2)}, u32[]{:S(2)}) %collective-permute-start.174) | collective-permute-done | bytes 1294368 | tf_op jit(solution)/shard_map/cond/branch_13_fun/ppermute | solution.py:233
  579.0 27.7 %collective-permute-done.176 = bf16[1264,512]{1,0:T(8,128)(2,1)} collective-permute-done((bf16[1264,512]{1,0:T(8,128)(2,1)S(1)}, bf16[1264,512]{1,0:T(8,128)(2,1)}, u32[]{:S(2)}, u32[]{:S(2)}) %collective-permute-start.176) | collective-permute-done | bytes 1294368 | tf_op jit(solution)/shard_map/cond/branch_13_fun/ppermute | solution.py:233
  606.7 27.7 %collective-permute-done.177 = bf16[1264,512]{1,0:T(8,128)(2,1)} collective-permute-done((bf16[1264,512]{1,0:T(8,128)(2,1)}, bf16[1264,512]{1,0:T(8,128)(2,1)}, u32[]{:S(2)}, u32[]{:S(2)}) %collective-permute-start.177) | collective-permute-done | bytes 1294368 | tf_op jit(solution)/shard_map/cond/branch_13_fun/ppermute | solution.py:233
  634.4 27.2 %collective-permute-done.178 = bf16[1264,512]{1,0:T(8,128)(2,1)} collective-permute-done((bf16[1264,512]{1,0:T(8,128)(2,1)}, bf16[1264,512]{1,0:T(8,128)(2,1)}, u32[]{:S(2)}, u32[]{:S(2)}) %collective-permute-start.178) | collective-permute-done | bytes 1294368 | tf_op jit(solution)/shard_map/cond/branch_13_fun/ppermute | solution.py:233
  661.6 10.4 %place_blocks.1 = (bf16[8192,512]{1,0:T(8,128)(2,1)}, bf16[256,512]{1,0:T(8,128)(2,1)}, bf16[512,4096]{1,0:T(8,128)(2,1)}, bf16[16,4096]{1,0:T(8,128)(2,1)}) custom-call(s32[1]{0:T(128)} %bitcast.15.choice_ref, bf16[8192,512]{1,0:T(8,128)(2,1)} %bitcast.42, bf16[256,512]{1,0:T(8,128)(2,1)} %bitcast.49, bf16[512,4096]{1,0:T(8,128)(2,1)} %bitcast.44, ...), custom_call_target="tpu_custom_call" | custom-call | tf_op jit(solution)/shard_map/place_blocks/pallas_call | solution.py:212
  (65 shorter events, 4.9 us)
Async XLA Ops:
  5.0 13.5 %collective-permute-start.190 = (bf16[16,4224]{1,0:T(8,128)(2,1)S(1)}, bf16[16,4224]{1,0:T(8,128)(2,1)S(1)}, u32[]{:S(2)}, u32[]{:S(2)}) collective-permute-start(bf16[16,4224]{1,0:T(8,128)(2,1)S(1)} %pad_maximum_fusion.2), channel_id=1, source_target_pairs={{0,24},{2,26},{4,28},{6,30},{8,16},{10,18},{12,20},{14,22},{16,8},... | collective-permute-start | bytes 405512 | tf_op jit(solution)/shard_map/ppermute | solution.py:36
  6.7 11.9 %collective-permute-start.189 = (bf16[16,4224]{1,0:T(8,128)(2,1)S(1)}, bf16[16,4224]{1,0:T(8,128)(2,1)S(1)}, u32[]{:S(2)}, u32[]{:S(2)}) collective-permute-start(bf16[16,4224]{1,0:T(8,128)(2,1)S(1)} %pad_maximum_fusion.2), channel_id=1, source_target_pairs={{0,16},{2,18},{4,20},{6,22},{8,24},{10,26},{12,28},{14,30},{16,0},... | collective-permute-start | bytes 405512 | tf_op jit(solution)/shard_map/ppermute | solution.py:36
  7.9 10.7 %collective-permute-start.188 = (bf16[16,4224]{1,0:T(8,128)(2,1)S(1)}, bf16[16,4224]{1,0:T(8,128)(2,1)S(1)}, u32[]{:S(2)}, u32[]{:S(2)}) collective-permute-start(bf16[16,4224]{1,0:T(8,128)(2,1)S(1)} %pad_maximum_fusion.2), channel_id=1, source_target_pairs={{0,8},{2,10},{4,12},{6,14},{8,0},{10,2},{12,4},{14,6},{16,24},{18,... | collective-permute-start | bytes 405512 | tf_op jit(solution)/shard_map/ppermute | solution.py:36
  18.6 27.5 %copy-start.20 = (bf16[1,2,128,512]{3,2,1,0:T(8,128)(2,1)S(1)}, bf16[1,2,128,512]{3,2,1,0:T(8,128)(2,1)}, u32[]{:S(2)}) copy-start(bf16[1,2,128,512]{3,2,1,0:T(8,128)(2,1)} %param.48) | copy-start | bytes 786436
  18.6 16.2 %collective-permute-start.193 = (bf16[64,4224]{1,0:T(8,128)(2,1)S(1)}, bf16[64,4224]{1,0:T(8,128)(2,1)S(1)}, u32[]{:S(2)}, u32[]{:S(2)}) collective-permute-start(bf16[64,4224]{1,0:T(8,128)(2,1)S(1)} %pad_maximum_fusion.1), channel_id=1, source_target_pairs={{0,6},{2,4},{4,2},{6,0},{8,14},{10,12},{12,10},{14,8},{16,22},{18,... | collective-permute-start | bytes 1622024 | tf_op jit(solution)/shard_map/ppermute | solution.py:36
  20.1 24.5 %collective-permute-start.192 = (bf16[64,4224]{1,0:T(8,128)(2,1)S(1)}, bf16[64,4224]{1,0:T(8,128)(2,1)S(1)}, u32[]{:S(2)}, u32[]{:S(2)}) collective-permute-start(bf16[64,4224]{1,0:T(8,128)(2,1)S(1)} %pad_maximum_fusion.1), channel_id=1, source_target_pairs={{0,4},{2,6},{4,0},{6,2},{8,12},{10,14},{12,8},{14,10},{16,20},{18,... | collective-permute-start | bytes 1622024 | tf_op jit(solution)/shard_map/ppermute | solution.py:36
  21.7 23.0 %collective-permute-start.191 = (bf16[64,4224]{1,0:T(8,128)(2,1)S(1)}, bf16[64,4224]{1,0:T(8,128)(2,1)S(1)}, u32[]{:S(2)}, u32[]{:S(2)}) collective-permute-start(bf16[64,4224]{1,0:T(8,128)(2,1)S(1)} %pad_maximum_fusion.1), channel_id=1, source_target_pairs={{0,2},{2,0},{4,6},{6,4},{8,10},{10,8},{12,14},{14,12},{16,18},{18,... | collective-permute-start | bytes 1622024 | tf_op jit(solution)/shard_map/ppermute | solution.py:36
  46.1 14.4 %collective-permute-start.194 = (bf16[256,4224]{1,0:T(8,128)(2,1)}, bf16[256,4224]{1,0:T(8,128)(2,1)}, u32[]{:S(2)}, u32[]{:S(2)}) collective-permute-start(bf16[256,4224]{1,0:T(8,128)(2,1)} %pad_maximum_fusion), channel_id=1, source_target_pairs={{0,1},{1,0},{2,3},{3,2},{4,5},{5,4},{6,7},{7,6},{8,9},{9,8},{10,11... | collective-permute-start | bytes 6488072 | tf_op jit(solution)/shard_map/ppermute | solution.py:36
  46.2 7.5 %copy-start.21 = (bf16[1,16,4096]{2,1,0:T(8,128)(2,1)S(1)}, bf16[1,16,4096]{2,1,0:T(8,128)(2,1)}, u32[]{:S(2)}) copy-start(bf16[1,16,4096]{2,1,0:T(8,128)(2,1)} %param.50) | copy-start | bytes 393220
  53.6 2.2 copy-start.18
  53.6 8.9 %slice-start = ((s8[8388608]{0:T(1024)(128)(4,1)}), s8[4194304]{0:T(1024)(128)(4,1)S(1)}, s32[]{:S(2)}) async-start(s8[8388608]{0:T(1024)(128)(4,1)} %bitcast.46), calls=%async_computation | async-start | bytes 8388608
  55.8 6.8 %slice-start.1 = ((s8[8388608]{0:T(1024)(128)(4,1)}), s8[4194304]{0:T(1024)(128)(4,1)S(1)}, s32[]{:S(2)}) async-start(s8[8388608]{0:T(1024)(128)(4,1)} %bitcast.46), calls=%async_computation.1 | async-start | bytes 8388608
  62.6 4.6 copy-start.19
  69.9 4.3 collective-permute-start.195
  75.0 3.7 copy-start
  75.2 25.6 %collective-permute-start.198 = (bf16[64,4096]{1,0:T(8,128)(2,1)S(1)}, bf16[64,4096]{1,0:T(8,128)(2,1)S(1)}, u32[]{:S(2)}, u32[]{:S(2)}) collective-permute-start(bf16[64,4096]{1,0:T(8,128)(2,1)S(1)} %get-tuple-element.724), channel_id=1, source_target_pairs={{0,6},{2,4},{4,2},{6,0},{8,14},{10,12},{12,10},{14,8},{16,22},{18,... | collective-permute-start | bytes 1572872 | tf_op jit(solution)/shard_map/ppermute | solution.py:36
  76.8 29.8 %collective-permute-start.197 = (bf16[64,4096]{1,0:T(8,128)(2,1)S(1)}, bf16[64,4096]{1,0:T(8,128)(2,1)S(1)}, u32[]{:S(2)}, u32[]{:S(2)}) collective-permute-start(bf16[64,4096]{1,0:T(8,128)(2,1)S(1)} %get-tuple-element.725), channel_id=1, source_target_pairs={{0,4},{2,6},{4,0},{6,2},{8,12},{10,14},{12,8},{14,10},{16,20},{18,... | collective-permute-start | bytes 1572872 | tf_op jit(solution)/shard_map/ppermute | solution.py:36
  77.5 34.8 %collective-permute-start.196 = (bf16[64,4096]{1,0:T(8,128)(2,1)S(1)}, bf16[64,4096]{1,0:T(8,128)(2,1)S(1)}, u32[]{:S(2)}, u32[]{:S(2)}) collective-permute-start(bf16[64,4096]{1,0:T(8,128)(2,1)S(1)} %get-tuple-element.723), channel_id=1, source_target_pairs={{0,2},{2,0},{4,6},{6,4},{8,10},{10,8},{12,14},{14,12},{16,18},{18,... | collective-permute-start | bytes 1572872 | tf_op jit(solution)/shard_map/ppermute | solution.py:36
  78.7 50.4 %collective-permute-start.203 = (bf16[1264,512]{1,0:T(8,128)(2,1)S(1)}, bf16[1264,512]{1,0:T(8,128)(2,1)S(1)}, u32[]{:S(2)}, u32[]{:S(2)}) collective-permute-start(bf16[1264,512]{1,0:T(8,128)(2,1)S(1)} %copy-done), channel_id=1, source_target_pairs={{0,2},{2,0},{4,6},{6,4},{8,10},{10,8},{12,14},{14,12},{16,18},{18,... | collective-permute-start | bytes 3883016 | tf_op jit(solution)/shard_map/ppermute | solution.py:14
  84.0 152.1 %copy-start.22 = (s32[8]{0:T(128)S(1)}, s32[8]{0:T(128)}, u32[]{:S(2)}) copy-start(s32[8]{0:T(128)} %param.51) | copy-start | bytes 100
  84.0 47.5 %collective-permute-start.206 = (bf16[1264,512]{1,0:T(8,128)(2,1)}, bf16[1264,512]{1,0:T(8,128)(2,1)S(1)}, u32[]{:S(2)}, u32[]{:S(2)}) collective-permute-start(bf16[1264,512]{1,0:T(8,128)(2,1)} %get-tuple-element.693), channel_id=1, source_target_pairs={{0,4},{2,6},{4,0},{6,2},{8,12},{10,14},{12,8},{14,10},{16,20},{18,... | collective-permute-start | bytes 3883016 | tf_op jit(solution)/shard_map/ppermute | solution.py:14
  100.8 137.4 %collective-permute-start.202 = (bf16[2560,512]{1,0:T(8,128)(2,1)}, bf16[2560,512]{1,0:T(8,128)(2,1)}, u32[]{:S(2)}, u32[]{:S(2)}) collective-permute-start(bf16[2560,512]{1,0:T(8,128)(2,1)} %get-tuple-element.689), channel_id=1, source_target_pairs={{0,16},{2,18},{4,20},{6,22},{8,24},{10,26},{12,28},{14,30},{16,0},... | collective-permute-start | bytes 7864328 | tf_op jit(solution)/shard_map/ppermute | solution.py:14
  106.6 131.6 %collective-permute-start.204 = (bf16[2528,512]{1,0:T(8,128)(2,1)S(1)}, bf16[2528,512]{1,0:T(8,128)(2,1)}, u32[]{:S(2)}, u32[]{:S(2)}) collective-permute-start(bf16[2528,512]{1,0:T(8,128)(2,1)S(1)} %get-tuple-element.691), channel_id=1, source_target_pairs={{0,2},{2,0},{4,6},{6,4},{8,10},{10,8},{12,14},{14,12},{16,18},{18,... | collective-permute-start | bytes 7766024 | tf_op jit(solution)/shard_map/ppermute | solution.py:14
  112.3 125.8 %collective-permute-start.208 = (bf16[2528,512]{1,0:T(8,128)(2,1)}, bf16[2528,512]{1,0:T(8,128)(2,1)}, u32[]{:S(2)}, u32[]{:S(2)}) collective-permute-start(bf16[2528,512]{1,0:T(8,128)(2,1)} %get-tuple-element.695), channel_id=1, source_target_pairs={{0,4},{2,6},{4,0},{6,2},{8,12},{10,14},{12,8},{14,10},{16,20},{18,... | collective-permute-start | bytes 7766024 | tf_op jit(solution)/shard_map/ppermute | solution.py:14
  129.1 1.1 copy-start.9
  130.1 100.4 %collective-permute-start.201 = (bf16[16,4096]{1,0:T(8,128)(2,1)S(1)}, bf16[16,4096]{1,0:T(8,128)(2,1)S(1)}, u32[]{:S(2)}, u32[]{:S(2)}) collective-permute-start(bf16[16,4096]{1,0:T(8,128)(2,1)S(1)} %get-tuple-element.727), channel_id=1, source_target_pairs={{0,24},{2,26},{4,28},{6,30},{8,16},{10,18},{12,20},{14,22},{16,8},... | collective-permute-start | bytes 393224 | tf_op jit(solution)/shard_map/ppermute | solution.py:36
  131.6 104.0 %copy-start.23 = (bf16[1264,512]{1,0:T(8,128)(2,1)}, bf16[1264,512]{1,0:T(8,128)(2,1)S(1)}, u32[]{:S(2)}) copy-start(bf16[1264,512]{1,0:T(8,128)(2,1)S(1)} %collective-permute-done.206) | copy-start | bytes 3883012
  131.6 99.3 %collective-permute-start.200 = (bf16[16,4096]{1,0:T(8,128)(2,1)S(1)}, bf16[16,4096]{1,0:T(8,128)(2,1)S(1)}, u32[]{:S(2)}, u32[]{:S(2)}) collective-permute-start(bf16[16,4096]{1,0:T(8,128)(2,1)S(1)} %get-tuple-element.728), channel_id=1, source_target_pairs={{0,16},{2,18},{4,20},{6,22},{8,24},{10,26},{12,28},{14,30},{16,0},... | collective-permute-start | bytes 393224 | tf_op jit(solution)/shard_map/ppermute | solution.py:36
  230.6 5.0 collective-permute-start.199
  230.9 30.7 %collective-permute-start.205 = (bf16[1264,512]{1,0:T(8,128)(2,1)}, bf16[1264,512]{1,0:T(8,128)(2,1)}, u32[]{:S(2)}, u32[]{:S(2)}) collective-permute-start(bf16[1264,512]{1,0:T(8,128)(2,1)} %get-tuple-element.692), channel_id=1, source_target_pairs={{0,2},{2,0},{4,6},{6,4},{8,10},{10,8},{12,14},{14,12},{16,18},{18,... | collective-permute-start | bytes 3883016 | tf_op jit(solution)/shard_map/ppermute | solution.py:14
  235.6 29.7 %collective-permute-start.207 = (bf16[1264,512]{1,0:T(8,128)(2,1)}, bf16[1264,512]{1,0:T(8,128)(2,1)}, u32[]{:S(2)}, u32[]{:S(2)}) collective-permute-start(bf16[1264,512]{1,0:T(8,128)(2,1)} %get-tuple-element.694), channel_id=1, source_target_pairs={{0,4},{2,6},{4,0},{6,2},{8,12},{10,14},{12,8},{14,10},{16,20},{18,... | collective-permute-start | bytes 3883016 | tf_op jit(solution)/shard_map/ppermute | solution.py:14
  267.3 20.9 %collective-permute-start.18 = (bf16[1264,512]{1,0:T(8,128)(2,1)}, bf16[1264,512]{1,0:T(8,128)(2,1)}, u32[]{:S(2)}, u32[]{:S(2)}) collective-permute-start(bf16[1264,512]{1,0:T(8,128)(2,1)} %get-tuple-element.442), channel_id=1, source_target_pairs={{6,20},{22,4},{7,21},{23,5}} | collective-permute-start | bytes 3883016 | tf_op jit(solution)/shard_map/cond/branch_4_fun/ppermute | solution.py:233
  274.8 15.2 %collective-permute-start.19 = (bf16[2528,512]{1,0:T(8,128)(2,1)}, bf16[2528,512]{1,0:T(8,128)(2,1)}, u32[]{:S(2)}, u32[]{:S(2)}) collective-permute-start(bf16[2528,512]{1,0:T(8,128)(2,1)} %get-tuple-element.443), channel_id=1, source_target_pairs={{6,20},{22,4},{7,21},{23,5}} | collective-permute-start | bytes 7766024 | tf_op jit(solution)/shard_map/cond/branch_4_fun/ppermute | solution.py:233
  282.7 7.3 %collective-permute-start.23 = (bf16[2528,512]{1,0:T(8,128)(2,1)}, bf16[2528,512]{1,0:T(8,128)(2,1)}, u32[]{:S(2)}, u32[]{:S(2)}) collective-permute-start(bf16[2528,512]{1,0:T(8,128)(2,1)} %get-tuple-element.447), channel_id=1, source_target_pairs={{0,20},{16,4},{1,21},{17,5}} | collective-permute-start | bytes 7766024 | tf_op jit(solution)/shard_map/cond/branch_4_fun/ppermute | solution.py:233
  284.9 5.1 collective-permute-start.20
  286.6 3.4 collective-permute-start.21
  288.3 1.7 collective-permute-start.22
  290.3 217.5 %collective-permute-start.179 = (bf16[2528,512]{1,0:T(8,128)(2,1)}, bf16[2528,512]{1,0:T(8,128)(2,1)}, u32[]{:S(2)}, u32[]{:S(2)}) collective-permute-start(bf16[2528,512]{1,0:T(8,128)(2,1)} %get-tuple-element.618), channel_id=1, source_target_pairs={{8,24},{24,8},{9,25},{25,9}} | collective-permute-start | bytes 7766024 | tf_op jit(solution)/shard_map/cond/branch_13_fun/ppermute | solution.py:233
  292.5 222.4 %collective-permute-start.180 = (bf16[2528,512]{1,0:T(8,128)(2,1)}, bf16[2528,512]{1,0:T(8,128)(2,1)}, u32[]{:S(2)}, u32[]{:S(2)}) collective-permute-start(bf16[2528,512]{1,0:T(8,128)(2,1)} %get-tuple-element.619), channel_id=1, source_target_pairs={{10,30},{26,14},{8,28},{24,12},{11,31},{27,15},{9,29},{25,13}} | collective-permute-start | bytes 7766024 | tf_op jit(solution)/shard_map/cond/branch_13_fun/ppermute | solution.py:233
  293.8 197.7 %copy-start.7 = (bf16[1264,512]{1,0:T(8,128)(2,1)S(1)}, bf16[1264,512]{1,0:T(8,128)(2,1)}, u32[]{:S(2)}) copy-start(bf16[1264,512]{1,0:T(8,128)(2,1)} %get-tuple-element.611) | copy-start | bytes 3883012 | tf_op jit(solution)/shard_map/cond
  293.8 197.7 %copy-start.16 = (bf16[1264,512]{1,0:T(8,128)(2,1)S(1)}, bf16[1264,512]{1,0:T(8,128)(2,1)}, u32[]{:S(2)}) copy-start(bf16[1264,512]{1,0:T(8,128)(2,1)} %get-tuple-element.610) | copy-start | bytes 3883012 | tf_op jit(solution)/shard_map/cond
  295.5 366.1 %collective-permute-start.175 = (bf16[2528,512]{1,0:T(8,128)(2,1)}, bf16[2528,512]{1,0:T(8,128)(2,1)}, u32[]{:S(2)}, u32[]{:S(2)}) collective-permute-start(bf16[2528,512]{1,0:T(8,128)(2,1)} %broadcast_select_fusion.25), channel_id=1, source_target_pairs={{10,24},{26,8},{14,30},{30,14},{12,28},{28,12},{11,25},{27,9},{15,... | collective-permute-start | bytes 7766024 | tf_op jit(solution)/shard_map/cond/branch_13_fun/ppermute | solution.py:233
  491.6 87.3 %collective-permute-start.174 = (bf16[1264,512]{1,0:T(8,128)(2,1)S(1)}, bf16[1264,512]{1,0:T(8,128)(2,1)}, u32[]{:S(2)}, u32[]{:S(2)}) collective-permute-start(bf16[1264,512]{1,0:T(8,128)(2,1)S(1)} %broadcast_select_fusion.27), channel_id=1, source_target_pairs={{10,24},{26,8},{14,30},{30,14},{12,28},{28,12},{11,25},{27,9},{15,... | collective-permute-start | bytes 3883016 | tf_op jit(solution)/shard_map/cond/branch_13_fun/ppermute | solution.py:233
  500.6 106.1 %collective-permute-start.176 = (bf16[1264,512]{1,0:T(8,128)(2,1)S(1)}, bf16[1264,512]{1,0:T(8,128)(2,1)}, u32[]{:S(2)}, u32[]{:S(2)}) collective-permute-start(bf16[1264,512]{1,0:T(8,128)(2,1)S(1)} %broadcast_select_fusion.26), channel_id=1, source_target_pairs={{10,24},{26,8},{14,30},{30,14},{12,28},{28,12},{11,25},{27,9},{15,... | collective-permute-start | bytes 3883016 | tf_op jit(solution)/shard_map/cond/branch_13_fun/ppermute | solution.py:233
  507.8 126.7 %collective-permute-start.177 = (bf16[1264,512]{1,0:T(8,128)(2,1)}, bf16[1264,512]{1,0:T(8,128)(2,1)}, u32[]{:S(2)}, u32[]{:S(2)}) collective-permute-start(bf16[1264,512]{1,0:T(8,128)(2,1)} %get-tuple-element.616), channel_id=1, source_target_pairs={{8,24},{24,8},{12,28},{28,12},{14,30},{30,14},{9,25},{25,9},{13,29... | collective-permute-start | bytes 3883016 | tf_op jit(solution)/shard_map/cond/branch_13_fun/ppermute | solution.py:233
  514.9 146.7 %collective-permute-start.178 = (bf16[1264,512]{1,0:T(8,128)(2,1)}, bf16[1264,512]{1,0:T(8,128)(2,1)}, u32[]{:S(2)}, u32[]{:S(2)}) collective-permute-start(bf16[1264,512]{1,0:T(8,128)(2,1)} %get-tuple-element.617), channel_id=1, source_target_pairs={{8,24},{24,8},{12,28},{28,12},{14,30},{30,14},{9,25},{25,9},{13,29... | collective-permute-start | bytes 3883016 | tf_op jit(solution)/shard_map/cond/branch_13_fun/ppermute | solution.py:233
